TPU v7x, 128 devices: a whole 4x4x4 slice. The times are simulated.
128 devices in a mesh: row: 8 (over z, core), col: 16 (over y, x).
Axes of the slice: x: 4, y: 4, z: 4, core: 2. Of those that a mesh axis runs over, the one named last changes fastest.
Arguments:
- lam_tiles: bfloat16 [128, 128, 16, 128], P(('row', 'col')), may hold values from -6 to 6
- lam_ids: int32 [128, 128], P(('row', 'col')), may hold values from 0 to 511, as said below
- integrals: bfloat16 [8192, 65536], P('row', 'col'), may hold values from -0.09375 to 0.09375
Outputs:
- ladder: float32 [2048, 8192], P('col', 'row')
Inputs may be any that keep to these rules, and one draw needn't show every extreme that they name: `lam_ids`: within a group the 128 ids are distinct; at most 16 of them lie in one block of 32 consecutive ids, and every group has exactly 16 in one block, the same block for all groups.
All inputs are finite; a program needn't handle non-finite values.
Results may differ from a plain program's by a relative error of at most 0.0003.
Values may be sent and summed in bfloat16 or wider, within the bound.
A program may use at most 128 MiB of HBM per device.

v0:
```python
import jax
import jax.numpy as jnp
from jax import lax
from jax.sharding import PartitionSpec as P

CAP = 16


def bucket_tiles(tiles, labels, target, n_dest, slots):
    onehot = (target[:, None] == jnp.arange(n_dest, dtype=jnp.int32)[None, :]).astype(jnp.int32)
    before = jnp.cumsum(onehot, axis=0) - onehot
    place = jnp.sum(before * onehot, axis=1)
    buffer = jnp.zeros((n_dest, slots) + tiles.shape[1:], tiles.dtype)
    buffer = buffer.at[target, place].set(tiles)
    marks = jnp.full((n_dest, slots), -1, jnp.int32).at[target, place].set(labels)
    return (buffer, marks)


def place_tiles(tiles, index, width):
    selector = (index[:, :, None] == jnp.arange(width, dtype=jnp.int32)[None, None, :]).astype(
        tiles.dtype
    )
    return jnp.einsum("nsw,nspt->nwpt", selector, tiles, preferred_element_type=jnp.bfloat16)


def shards(lam_tiles, lam_ids, integrals):
    n_row = lax.axis_size("row")
    n_col = lax.axis_size("col")
    g_dev, s_count, pairs, tile = lam_tiles.shape
    ab_dev = integrals.shape[0]
    kt_dev = integrals.shape[1] // tile
    groups = g_dev * n_row * n_col
    first = (lax.axis_index("row") * n_col + lax.axis_index("col")) * g_dev
    owned = first + lax.broadcasted_iota(jnp.int32, (g_dev, s_count), 0)
    labels = owned * kt_dev + lam_ids % kt_dev
    target = lam_ids // kt_dev
    buffer, marks = bucket_tiles(
        lam_tiles.reshape(-1, pairs, tile),
        labels.reshape(-1),
        target.reshape(-1),
        n_col,
        g_dev * CAP,
    )
    got_tiles, got_marks = (
        lax.all_to_all(buffer, "col", split_axis=0, concat_axis=0, tiled=True),
        lax.all_to_all(marks, "col", split_axis=0, concat_axis=0, tiled=True),
    )
    piece_tiles = lax.all_gather(got_tiles[None], "row", axis=0, tiled=True)
    piece_marks = lax.all_gather(got_marks[None], "row", axis=0, tiled=True)
    sources = piece_marks.shape[0] * piece_marks.shape[1]
    flat_marks = piece_marks.reshape(sources, piece_marks.shape[2])
    flat_tiles = piece_tiles.reshape((sources,) + piece_tiles.shape[2:])
    source = lax.broadcasted_iota(jnp.int32, flat_marks.shape, 0)
    index = jnp.where(flat_marks >= 0, flat_marks - source * (g_dev * kt_dev), -1)
    built = place_tiles(flat_tiles, index, g_dev * kt_dev)
    columns = integrals.reshape(ab_dev, kt_dev, tile)
    product = jnp.einsum("gkpt,akt->gpa", built, columns, preferred_element_type=jnp.float32)
    return lax.psum_scatter(
        0.5 * product.reshape(groups * pairs // n_col * lax.axis_size("col"), ab_dev),
        "col",
        scatter_dimension=0,
        tiled=True,
    )


def solution(mesh):
    return jax.shard_map(
        shards,
        mesh=mesh,
        in_specs=(P(("row", "col"), None, None, None), P(("row", "col"), None), P("row", "col")),
        out_specs=P("col", "row"),
        check_vma=False,
    )
```

profile of v0, /device:TPU:22, one launch (start us, length us, event | category | flops | bytes accessed | tf_op | source)
XLA Modules:
  0.0 218.9 jit_solution(13672670768527329519)
XLA Ops:
  6.5 0.0 all-gather.4.cloned.1.call-start
  6.5 0.7 fusion.17
  7.2 0.1 fusion.14
  7.3 0.2 reduce_window_sum.11
  7.5 0.2 select_reduce_fusion
  7.7 0.2 broadcast_in_dim.26
  7.9 8.8 %scatter_fusion.1 = bf16[16,16,16,128]{3,2,1,0:T(8,128)(2,1)S(1)} fusion(bf16[16,16,16,128]{3,2,1,0:T(8,128)(2,1)S(1)} %broadcast_in_dim.26, s32[128]{0:T(128)S(1)} %fusion.18, bf16[128,16,128]{2,1,0:T(8,128)(2,1)} %bitcast.47), kind=kCustom, calls=%fused_computation.1 | custom fusion | bytes 1573888 | tf_op jit(solution)/shard_map/scatter | solution.py:14
  16.6 20.2 %all_to_all.14 = bf16[16,16,16,128]{3,2,1,0:T(8,128)(2,1)} all-to-all(bf16[16,16,16,128]{3,2,1,0:T(8,128)(2,1)S(1)} %scatter_fusion.1), channel_id=1, replica_groups=mesh['row'=8,'col'=16] {'col'}, dimensions={0} | all-to-all | bytes 2097152 | tf_op jit(solution)/shard_map/all_to_all | solution.py:45
  36.8 0.0 all-gather.4.cloned.1.call-update
  36.8 0.6 broadcast_in_dim.12
  37.4 18.7 %scatter_fusion = s32[16,16]{1,0:T(8,128)} fusion(s32[16,16]{1,0:T(8,128)} %broadcast_in_dim.12, s32[128]{0:T(128)S(1)} %fusion.18, s32[128]{0:T(128)S(1)} %get-tuple-element.5), kind=kCustom, calls=%fused_computation | custom fusion | bytes 2560 | tf_op jit(solution)/shard_map/scatter | solution.py:15
  56.1 7.6 %all-to-all-start = ((s32[16,1,16]{2,1,0:T(1,128)}), s32[16,1,16]{2,1,0:T(1,128)S(1)}, u32[]{:S(2)}, u32[]{:S(2)}) async-start(s32[16,1,16]{2,1,0:T(1,128)} %bitcast.6), calls=%async_computation | async-start | bytes 16384 | tf_op jit(solution)/shard_map/all_to_all | solution.py:46
  63.7 0.0 reduce-scatter.2.cloned.1.call-start
  63.7 3.7 %all-to-all-done = s32[16,1,16]{2,1,0:T(1,128)S(1)} async-done(((s32[16,1,16]{2,1,0:T(1,128)}), s32[16,1,16]{2,1,0:T(1,128)S(1)}, u32[]{:S(2)}, u32[]{:S(2)}) %all-to-all-start) | async-done | bytes 1056 | tf_op jit(solution)/shard_map/all_to_all | solution.py:46
  67.4 14.5 %all-gather = s32[128,1,16]{2,0,1:T(8,128)S(1)} all-gather(s32[16,1,16]{2,0,1:T(8,128)S(1)} %bitcast.48), channel_id=2, replica_groups=mesh['row'=8,'col'=16] {'row'}, dimensions={0}, use_global_device_ids=true | all-gather | bytes 9216 | tf_op jit(solution)/shard_map/all_gather | solution.py:49
  81.9 0.1 fusion.13
  82.0 7.3 %all-gather.4.cloned.1.call-done = bf16[128,16,16,128]{3,2,1,0:T(8,128)(2,1)} async-done(((bf16[16,16,16,128]{3,2,1,0:T(8,128)(2,1)}), bf16[128,16,16,128]{3,2,1,0:T(8,128)(2,1)}) %all-gather.4.cloned.1.call-update) | async-done | bytes 8388624 | tf_op jit(solution)/shard_map/all_gather | solution.py:48
  89.3 13.0 %fusion.4 = bf16[128,32,16,128]{3,1,2,0:T(8,128)(2,1)} fusion(bf16[128,16,16,128]{3,2,1,0:T(8,128)(2,1)} %all-gather.4.cloned.1.call-done, s32[128,16]{1,0:T(8,128)S(1)} %fusion.13), kind=kOutput, calls=%fused_computation.7 | convolution fusion | flops 268500992 | bytes 25174016 | tf_op jit(solution)/shard_map/nsw,nspt->nwpt/dot_general | solution.py:23
  102.3 25.6 %bitcast_multiply_fusion = f32[2048,1024]{1,0:T(8,128)} fusion(bf16[2048,32,128]{2,1,0:T(8,128)(2,1)} %bitcast.46, bf16[1024,4096]{1,0:T(8,128)(2,1)} %param.5), kind=kOutput, calls=%fused_computation.6 | convolution fusion | flops 17181966336 | bytes 33554432 | tf_op jit(solution)/shard_map/gkpt,akt->gpa/dot_general | solution.py:57
  127.9 0.0 reduce-scatter.2.cloned.1.call-update
  128.0 84.1 %reduce-scatter.2.cloned.1.call-done = f32[128,1024]{1,0:T(8,128)} async-done(((f32[2048,1024]{1,0:T(8,128)}), f32[128,1024]{1,0:T(8,128)}) %reduce-scatter.2.cloned.1.call-update) | async-done | bytes 524304 | tf_op jit(solution)/shard_map/reduce_scatter | solution.py:58
  (2 shorter events, 0.0 us)
Async XLA Ops:
  6.5 82.8 %all-gather.4.cloned.1.call-start = ((), (), s32[]{:S(2)}) async-start(), calls=%async_computation.4 | async-start | bytes 9437184 | tf_op jit(solution)/shard_map/all_gather | solution.py:48
  56.1 11.3 %all-to-all-start = ((s32[16,1,16]{2,1,0:T(1,128)}), s32[16,1,16]{2,1,0:T(1,128)S(1)}, u32[]{:S(2)}, u32[]{:S(2)}) async-start(s32[16,1,16]{2,1,0:T(1,128)} %bitcast.6), calls=%async_computation | async-start | bytes 16384 | tf_op jit(solution)/shard_map/all_to_all | solution.py:46
  63.7 148.4 %reduce-scatter.2.cloned.1.call-start = ((), (), s32[]{:S(2)}) async-start(), calls=%async_computation.3 | async-start | bytes 8912896 | tf_op jit(solution)/shard_map/reduce_scatter | solution.py:58
Sparse Core Ops, SparseCore 0:
  37.0 52.2 all-gather.3
  128.1 83.9 reduce-scatter.1
where the time goes:
time: 222 us; the launch traced here: 219 us
  waiting for transfers between devices  95.1 us (43%)
  matrix products  38.6 us (17%)
  blocking collectives  34.6 us (16%)
  local copies, waits for them, and re-layouts  28.2 us (13%)
  between operations  13.5 us (6%)
  starting transfers between devices  7.61 us (3%)
    reduce_scatter x1, waiting for transfers between devices, shards(): lax.psum_scatter(0.5 * product.reshape(groups * pairs // n_col * lax.axis...  84.1 us
    dot_general x1, matrix products, shards(): jnp.einsum('gkpt,akt->gpa', built, columns, preferred_element_type=jnp.fl...  25.6 us
    all_to_all x1, blocking collectives, shards(): lax.all_to_all(buffer, 'col', split_axis=0, concat_axis=0, tiled=True)  20.2 us
    scatter x1, local copies, waits for them, and re-layouts, bucket_tiles(): jnp.full((n_dest, slots), -1, jnp.int32).at[target, place].set(labels)  18.7 us
    all_gather x1, blocking collectives, shards(): piece_marks = lax.all_gather(got_marks[None], 'row', axis=0, tiled=True)  14.5 us
    dot_general x1, matrix products, place_tiles(): jnp.einsum('nsw,nspt->nwpt', selector, tiles, preferred_element_type=jnp....  13 us
    scatter x1, local copies, waits for them, and re-layouts, bucket_tiles(): buffer = buffer.at[target, place].set(tiles)  8.77 us
    all_to_all x1, starting transfers between devices, shards(): lax.all_to_all(marks, 'col', split_axis=0, concat_axis=0, tiled=True)  7.58 us
  transfers between devices with their start and end apart: 3, of which 3 were waited for; matrix products, arithmetic and copies ran while one was open for 9% of the time, Pallas kernels for 0%

commit v1 on v0

v1 whole, which is shorter than its diff:
```python
import functools

import jax
import jax.numpy as jnp
from jax import lax
from jax.experimental import pallas as pl
from jax.experimental.pallas import tpu as pltpu
from jax.sharding import PartitionSpec as P

CAP = 16
MESH = pl.DeviceIdType.MESH
DYS = (0, 1, 3, 2)
NT = (((1,), (1,)), ((), ()))
OWN, PART, ZM, ZP, PZM, PZP, Z2, PZ2 = range(8)
STEPS = (OWN, PART, ZM, ZP, PZM, PZP, Z2, PZ2)
OFFSET = {OWN: 0, PART: 0, ZM: 3, PZM: 3, ZP: 1, PZP: 1, Z2: 2, PZ2: 2}


def bucket_kernel(place_ref, lam_ref, out_ref):
    def body(s, carry):
        out_ref[place_ref[s]] = lam_ref[s]
        return carry

    lax.fori_loop(0, lam_ref.shape[0], body, 0, unroll=8)


def bucket(place, tiles, slots):
    return pl.pallas_call(
        bucket_kernel,
        out_shape=jax.ShapeDtypeStruct((slots,) + tiles.shape[1:], tiles.dtype),
        in_specs=[
            pl.BlockSpec(memory_space=pltpu.SMEM),
            pl.BlockSpec(memory_space=pltpu.VMEM),
        ],
        out_specs=pl.BlockSpec(memory_space=pltpu.VMEM),
        name="bucket",
    )(place, tiles)


def wide(scale, width):
    return jnp.concatenate([jnp.concatenate([scale, scale], axis=0)] * (width // 128), axis=1)


def quantize(src, dst, scale_dst):
    rows, width = src.shape

    def largest(r, m):
        a = jnp.abs(src[pl.ds(r * 16, 16), :])
        for j in range(width // 128):
            part = a[:, j * 128 : (j + 1) * 128]
            m = jnp.maximum(m, jnp.maximum(part[:8], part[8:]))
        return m

    m = lax.fori_loop(0, rows // 16, largest, jnp.zeros((8, 128), jnp.float32), unroll=2)
    scale_dst[...] = m * (1.0 / 32767.0)
    inverse = wide(jnp.where(m > 0.0, 32767.0 / m, 0.0), width)

    def code(r, carry):
        at = pl.ds(pl.multiple_of(r * 16, 16), 16)
        dst[at, :] = jnp.round(src[at, :] * inverse).astype(jnp.int32).astype(jnp.int16)
        return carry

    lax.fori_loop(0, rows // 16, code, 0, unroll=2)


def add_coded(acc, coded, scales, factor=None, out=None):
    rows, width = acc.shape
    w = [wide(scales[j], width) for j in range(3)]

    def body(r, carry):
        at = pl.ds(pl.multiple_of(r * 16, 16), 16)
        total = acc[at, :]
        for j in range(3):
            total = total + coded[j, at, :].astype(jnp.int32).astype(jnp.float32) * w[j]
        if out is None:
            acc[at, :] = total
        else:
            out[at, :] = factor * total
        return carry

    lax.fori_loop(0, rows // 16, body, 0, unroll=2)


def ladder_kernel(
    buf_ref, inv_ref, int_ref, out_ref,
    r0, r1, r2, r3, r4, r5, r6, r7, tabs, smem, ints, dense, prod,
    q1, s1, q2, s2, q3, s3, q4, s4,
    rq1, rs1, rq2, rs2, rq3, rs3, rq4, rs4,
    acc1, acc2, fin1, fin2,
    int_sem, smem_sem, loc_sem,
    ta_send, ta_recv, t_send, t_recv,
    a_send, a_recv, b_send, b_recv, c_send, c_recv, d_send, d_recv,
    q1_send, q1_recv, q2_send, q2_recv, q3_send, q3_recv, q4_send, q4_recv,
    s1_send, s1_recv, s2_send, s2_recv, s3_send, s3_recv, s4_send, s4_recv,
):
    rbuf = (r0, r1, r2, r3, r4, r5, r6, r7)
    row, col = lax.axis_index("row"), lax.axis_index("col")
    z, core = row // 2, row % 2
    y, x = col // 4, col % 4
    up = ((z + 1) % 4) * 2 + core
    down = ((z + 3) % 4) * 2 + core
    partner = z * 2 + (1 - core)

    barrier = pltpu.get_barrier_semaphore()

    def greet(j, carry):
        pl.semaphore_signal(barrier, inc=1, device_id={"row": row, "col": (col + j) % 16}, device_id_type=MESH)
        return carry

    lax.fori_loop(1, 16, greet, 0)
    for other in (up, down, partner):
        pl.semaphore_signal(barrier, inc=1, device_id={"row": other, "col": col}, device_id_type=MESH)
    pl.semaphore_wait(barrier, 18)

    def remote(src, dst, send, recv, to_row, to_col):
        return pltpu.make_async_remote_copy(
            src_ref=src, dst_ref=dst, send_sem=send, recv_sem=recv,
            device_id={"row": to_row, "col": to_col}, device_id_type=MESH,
        )

    def wait_bytes(ref, sem):
        pltpu.make_async_copy(ref, ref, sem).wait()

    load = pltpu.make_async_copy(int_ref, ints, int_sem)

    mine = pl.ds(col, 1)
    own_table = pltpu.make_async_copy(inv_ref.at[mine], tabs.at[OWN, mine], ta_recv)
    own_table.start()

    def send_table(j, carry):
        to = (col + j) % 16
        remote(inv_ref.at[pl.ds(to, 1)], tabs.at[OWN, mine], ta_send.at[j], ta_recv, row, to).start()
        return carry

    lax.fori_loop(1, 16, send_table, 0)

    here = pl.ds(pl.multiple_of(col * CAP, CAP), CAP)
    pltpu.make_async_copy(buf_ref.at[here], r0.at[here], a_recv.at[0]).start()

    def tile_copy(dy, j):
        to = ((y + 4 - dy) % 4) * 4 + (x + j) % 4
        there = pl.ds(pl.multiple_of(to * CAP, CAP), CAP)
        return remote(buf_ref.at[there], r0.at[here], a_send.at[dy * 4 + j], a_recv.at[dy], row, to)

    for dy in DYS:
        for j in range(1 if dy == 0 else 0, 4):
            tile_copy(dy, j).start()
    load.start()

    zero = jnp.zeros((16, 128), jnp.bfloat16)
    for r in rbuf:
        r[16 * CAP] = zero

    wait_bytes(tabs.at[OWN], ta_recv)
    t_own = [
        remote(tabs.at[OWN], tabs.at[ZM], t_send.at[0], t_recv.at[ZM], up, col),
        remote(tabs.at[OWN], tabs.at[ZP], t_send.at[1], t_recv.at[ZP], down, col),
        remote(tabs.at[OWN], tabs.at[PART], t_send.at[2], t_recv.at[PART], partner, col),
    ]
    for t in t_own:
        t.start()

    def quarter(dy):
        return pl.ds(pl.multiple_of(((y + dy) % 4) * 4 * CAP, 4 * CAP), 4 * CAP)

    def b_copies(dy):
        at = quarter(dy)
        return [
            remote(r0.at[at], rbuf[ZM].at[at], b_send.at[0, dy], b_recv.at[0, dy], up, col),
            remote(r0.at[at], rbuf[ZP].at[at], b_send.at[1, dy], b_recv.at[1, dy], down, col),
            remote(r0.at[at], rbuf[PART].at[at], b_send.at[2, dy], b_recv.at[2, dy], partner, col),
        ]

    def c_copy(dy):
        at = quarter(dy)
        if dy in (0, 3):
            return remote(rbuf[ZP].at[at], rbuf[Z2].at[at], c_send.at[dy], c_recv.at[dy], down, col)
        return remote(rbuf[ZM].at[at], rbuf[Z2].at[at], c_send.at[dy], c_recv.at[dy], up, col)

    def d_copy(which, dy):
        at = quarter(dy)
        src, dst = ((ZM, PZM), (ZP, PZP), (Z2, PZ2))[which]
        return remote(rbuf[src].at[at], rbuf[dst].at[at], d_send.at[which, dy], d_recv.at[which, dy], partner, col)

    for dy in DYS:
        wait_bytes(r0.at[quarter(dy)], a_recv.at[dy])
        for copy in b_copies(dy):
            copy.start()

    def arrived(buf, sem, dys=DYS):
        for dy in dys:
            wait_bytes(rbuf[buf].at[quarter(dy)], sem.at[dy])

    def where_from(step):
        zi = (z + OFFSET[step]) % 4
        ki = core if step in (OWN, ZM, ZP, Z2) else 1 - core
        return zi, ki

    def compute(step):
        fetch = pltpu.make_async_copy(tabs.at[step], smem, smem_sem)
        fetch.start()
        fetch.wait()
        tiles = rbuf[step]

        def build(g, carry):
            for k in range(32):
                dense[pl.ds(pl.multiple_of(g * 16, 16), 16), k * 128 : (k + 1) * 128] = tiles[smem[g, 0, k]]
            return carry

        lax.fori_loop(0, 16, build, 0)

        def columns(n, carry):
            at = pl.ds(pl.multiple_of(n * 256, 256), 256)
            prod[:, at] = lax.dot_general(dense[...], ints[at, :], NT, preferred_element_type=jnp.float32)
            return carry

        lax.fori_loop(0, 4, columns, 0)

    def q1_copies(step):
        zi, ki = where_from(step)
        d = (y + 3 - zi) % 4
        to = zi * 4 + x
        return (
            remote(q1.at[step], rq1.at[ki, d], q1_send.at[step], q1_recv.at[ki, d], row, to),
            remote(s1.at[step], rs1.at[ki, d], s1_send.at[step], s1_recv.at[ki, d], row, to),
        )

    def q2_copies(step, e):
        zi, ki = where_from(step)
        xd = 2 * ki + e
        d = (x + 3 - xd) % 4
        to = y * 4 + xd
        return (
            remote(q2.at[step, e], rq2.at[zi, d], q2_send.at[step, e], q2_recv.at[zi, d], row, to),
            remote(s2.at[step, e], rs2.at[zi, d], s2_send.at[step, e], s2_recv.at[zi, d], row, to),
        )

    def q3_copies(step, e):
        zi, ki = where_from(step)
        xd = 2 * ki + e
        d = (x + 3 - xd) % 4
        to = zi * 4 + xd
        return (
            remote(q3.at[ki, e], rq3.at[d], q3_send.at[ki, e], q3_recv.at[d], row, to),
            remote(s3.at[ki, e], rs3.at[d], s3_send.at[ki, e], s3_recv.at[d], row, to),
        )

    def q4_copies(step):
        zi, ki = where_from(step)
        d = (y + 3 - zi) % 4
        to = zi * 4 + x
        return (
            remote(q4.at[zi], rq4.at[d], q4_send.at[zi], q4_recv.at[d], row, to),
            remote(s4.at[zi], rs4.at[d], s4_send.at[zi], s4_recv.at[d], row, to),
        )

    def move(src, dst):
        rows = src.shape[0]

        def body(r, carry):
            at = pl.ds(pl.multiple_of(r * 16, 16), 16)
            dst[at, :] = src[at, :]
            return carry

        lax.fori_loop(0, rows // 16, body, 0)

    def first_sends(step):
        zi, ki = where_from(step)
        left, right = prod.at[:, pl.ds(0, 512)], prod.at[:, pl.ds(512, 512)]

        @pl.when(y != zi)
        def _():
            quantize(left, q1.at[step], s1.at[step])
            for copy in q1_copies(step):
                copy.start()

        @pl.when(y == zi)
        def _():
            move(left, acc1.at[ki])

        for e in range(2):
            part = right.at[pl.ds(e * 128, 128), :]

            @pl.when(x != 2 * ki + e)
            def _():
                quantize(part, q2.at[step, e], s2.at[step, e])
                for copy in q2_copies(step, e):
                    copy.start()

            @pl.when(x == 2 * ki + e)
            def _():
                move(part, acc2.at[zi])

    def second_sends(step):
        zi, ki = where_from(step)

        @pl.when(y == zi)
        def _():
            for d in range(3):
                wait_bytes(rq1.at[ki, d], q1_recv.at[ki, d])
                wait_bytes(rs1.at[ki, d], s1_recv.at[ki, d])
            add_coded(acc1.at[ki], rq1.at[ki], rs1.at[ki])
            for e in range(2):
                part = acc1.at[ki, pl.ds(e * 128, 128), :]

                @pl.when(x != 2 * ki + e)
                def _():
                    quantize(part, q3.at[ki, e], s3.at[ki, e])
                    for copy in q3_copies(step, e):
                        copy.start()

                @pl.when(x == 2 * ki + e)
                def _():
                    move(part, fin1)

        @pl.when(x // 2 == ki)
        def _():
            for d in range(3):
                wait_bytes(rq2.at[zi, d], q2_recv.at[zi, d])
                wait_bytes(rs2.at[zi, d], s2_recv.at[zi, d])
            add_coded(acc2.at[zi], rq2.at[zi], rs2.at[zi])

            @pl.when(y != zi)
            def _():
                quantize(acc2.at[zi], q4.at[zi], s4.at[zi])
                for copy in q4_copies(step):
                    copy.start()

            @pl.when(y == zi)
            def _():
                move(acc2.at[zi], fin2)

    load.wait()
    compute(OWN)
    first_sends(OWN)

    wait_bytes(tabs.at[ZM], t_recv.at[ZM])
    wait_bytes(tabs.at[ZP], t_recv.at[ZP])
    t_more = [
        remote(tabs.at[ZP], tabs.at[Z2], t_send.at[3], t_recv.at[Z2], down, col),
        remote(tabs.at[ZM], tabs.at[PZM], t_send.at[4], t_recv.at[PZM], partner, col),
        remote(tabs.at[ZP], tabs.at[PZP], t_send.at[5], t_recv.at[PZP], partner, col),
    ]
    for t in t_more:
        t.start()

    def pass_on(dys):
        for dy in dys:
            wait_bytes(rbuf[ZM].at[quarter(dy)], b_recv.at[0, dy])
            wait_bytes(rbuf[ZP].at[quarter(dy)], b_recv.at[1, dy])
            c_copy(dy).start()
            d_copy(0, dy).start()
            d_copy(1, dy).start()

    pass_on(DYS[:2])
    wait_bytes(tabs.at[PART], t_recv.at[PART])
    arrived(PART, b_recv.at[2])
    compute(PART)
    first_sends(PART)
    second_sends(OWN)
    pass_on(DYS[2:])

    compute(ZM)
    first_sends(ZM)
    second_sends(PART)

    wait_bytes(tabs.at[Z2], t_recv.at[Z2])
    t_last = remote(tabs.at[Z2], tabs.at[PZ2], t_send.at[6], t_recv.at[PZ2], partner, col)
    t_last.start()

    compute(ZP)
    first_sends(ZP)
    second_sends(ZM)

    def pass_far(dys):
        for dy in dys:
            wait_bytes(rbuf[Z2].at[quarter(dy)], c_recv.at[dy])
            d_copy(2, dy).start()

    wait_bytes(tabs.at[PZM], t_recv.at[PZM])
    arrived(PZM, d_recv.at[0])
    compute(PZM)
    first_sends(PZM)
    second_sends(ZP)
    pass_far(DYS[:2])

    wait_bytes(tabs.at[PZP], t_recv.at[PZP])
    arrived(PZP, d_recv.at[1])
    compute(PZP)
    first_sends(PZP)
    second_sends(PZM)
    pass_far(DYS[2:])

    compute(Z2)
    first_sends(Z2)
    second_sends(PZP)

    wait_bytes(tabs.at[PZ2], t_recv.at[PZ2])
    arrived(PZ2, d_recv.at[2])
    compute(PZ2)
    first_sends(PZ2)
    second_sends(Z2)
    second_sends(PZ2)

    for d in range(3):
        wait_bytes(rq3.at[d], q3_recv.at[d])
        wait_bytes(rs3.at[d], s3_recv.at[d])
    add_coded(fin1, rq3, rs3, 0.5, out_ref.at[:, pl.ds(0, 512)])
    for d in range(3):
        wait_bytes(rq4.at[d], q4_recv.at[d])
        wait_bytes(rs4.at[d], s4_recv.at[d])
    add_coded(fin2, rq4, rs4, 0.5, out_ref.at[:, pl.ds(512, 512)])

    def table_left(j, carry):
        remote(inv_ref.at[mine], tabs.at[OWN, mine], ta_send.at[j], ta_recv, row, (col + j) % 16).wait_send()
        return carry

    lax.fori_loop(1, 16, table_left, 0)
    for t in t_own + t_more + [t_last]:
        t.wait_send()
    for dy in DYS:
        for j in range(1 if dy == 0 else 0, 4):
            tile_copy(dy, j).wait_send()
        for copy in b_copies(dy):
            copy.wait_send()
        c_copy(dy).wait_send()
        for which in range(3):
            d_copy(which, dy).wait_send()
    for step in STEPS:
        zi, ki = where_from(step)

        @pl.when(y != zi)
        def _():
            for copy in q1_copies(step):
                copy.wait_send()

        for e in range(2):

            @pl.when(x != 2 * ki + e)
            def _():
                for copy in q2_copies(step, e):
                    copy.wait_send()

            @pl.when((y == zi) & (x != 2 * ki + e))
            def _():
                for copy in q3_copies(step, e):
                    copy.wait_send()

        @pl.when((y != zi) & (x // 2 == ki))
        def _():
            for copy in q4_copies(step):
                copy.wait_send()


def ladder(buf, inv, integrals):
    ab, cd = integrals.shape
    half = ab // 2
    i16, f32, bf16 = jnp.int16, jnp.float32, jnp.bfloat16
    dma = pltpu.SemaphoreType.DMA
    vmem = pltpu.VMEM
    scratch = [vmem((16 * CAP + 1, 16, 128), bf16) for _ in range(8)]
    scratch += [
        vmem((8, 16, 1, 128), jnp.int32), pltpu.SMEM((16, 1, 128), jnp.int32),
        vmem((ab, cd), bf16), vmem((256, cd), bf16), vmem((256, ab), f32),
        vmem((8, 256, half), i16), vmem((8, 8, 128), f32),
        vmem((8, 2, 128, half), i16), vmem((8, 2, 8, 128), f32),
        vmem((2, 2, 128, half), i16), vmem((2, 2, 8, 128), f32),
        vmem((4, 128, half), i16), vmem((4, 8, 128), f32),
        vmem((2, 3, 256, half), i16), vmem((2, 3, 8, 128), f32),
        vmem((4, 3, 128, half), i16), vmem((4, 3, 8, 128), f32),
        vmem((3, 128, half), i16), vmem((3, 8, 128), f32),
        vmem((3, 128, half), i16), vmem((3, 8, 128), f32),
        vmem((2, 256, half), f32), vmem((4, 128, half), f32),
        vmem((128, half), f32), vmem((128, half), f32),
        dma, dma, dma,
        dma((16,)), dma, dma((7,)), dma((8,)),
        dma((16,)), dma((4,)), dma((3, 4)), dma((3, 4)), dma((4,)), dma((4,)), dma((3, 4)), dma((3, 4)),
        dma((8,)), dma((2, 3)), dma((8, 2)), dma((4, 3)), dma((2, 2)), dma((3,)), dma((4,)), dma((3,)),
        dma((8,)), dma((2, 3)), dma((8, 2)), dma((4, 3)), dma((2, 2)), dma((3,)), dma((4,)), dma((3,)),
    ]
    any_space = pl.BlockSpec(memory_space=pl.ANY)
    return pl.pallas_call(
        ladder_kernel,
        out_shape=jax.ShapeDtypeStruct((128, ab), f32),
        in_specs=[any_space, any_space, any_space],
        out_specs=pl.BlockSpec(memory_space=pltpu.VMEM),
        scratch_shapes=scratch,
        compiler_params=pltpu.CompilerParams(collective_id=0, has_side_effects=True, vmem_limit_bytes=60 << 20),
        name="ladder",
    )(buf, inv, integrals)


def tables(ids, col, n_col, kt_dev):
    block = ids // kt_dev
    lower = (block[:, None] == block[None, :]) & (ids[None, :] < ids[:, None])
    place = block * CAP + jnp.sum(lower.astype(jnp.int32), axis=1)
    tile = jnp.arange(n_col * kt_dev, dtype=jnp.int32)
    present = jnp.any(ids[None, :] == tile[:, None], axis=1)
    before = (block[None, :] == (tile // kt_dev)[:, None]) & (ids[None, :] < tile[:, None])
    rank = jnp.sum(before.astype(jnp.int32), axis=1)
    inv = jnp.where(present, col * CAP + rank, n_col * CAP).reshape(n_col, 1, kt_dev)
    return place, jnp.pad(inv, ((0, 0), (0, 0), (0, 128 - kt_dev)))


def shards(lam_tiles, lam_ids, integrals):
    n_col = lax.axis_size("col")
    _, s_count, pairs, tile = lam_tiles.shape
    kt_dev = integrals.shape[1] // tile
    place, inv = tables(lam_ids.reshape(-1), lax.axis_index("col"), n_col, kt_dev)
    buf = bucket(place, lam_tiles.reshape(s_count, pairs, tile), n_col * CAP)
    return ladder(buf, inv, integrals)


def solution(mesh):
    return jax.shard_map(
        shards,
        mesh=mesh,
        in_specs=(P(("row", "col"), None, None, None), P(("row", "col"), None), P("row", "col")),
        out_specs=P("col", "row"),
        check_vma=False,
    )
```

time: 222 us -> 120 us (0.54); the launches traced: 219 us -> 119 us
  Pallas kernels: 0 us -> 112 us
  waiting for transfers between devices: 95.1 us -> 0 us
  matrix products: 38.6 us -> 0 us
  blocking collectives: 34.6 us -> 0 us
  local copies, waits for them, and re-layouts: 28.2 us -> 2.58 us
  between operations: 13.5 us -> 0.02 us
  starting transfers between devices: 7.61 us -> 0 us
  other arithmetic: 1.18 us -> 5.19 us
    pallas_call x0 -> x2, Pallas kernels: none -> 112 us  [the longest x1 109 us: ladder(): pl.pallas_call(ladder_kernel, out_shape=jax.ShapeDtypeStruct((128, ab), f...]
    reduce_scatter x1 -> x0, waiting for transfers between devices: 84.1 us -> none  [shards(): lax.psum_scatter(0.5 * product.reshape(groups * pairs // n_col * lax.axis...]
    dot_general x2 -> x0, matrix products: 38.6 us -> none  [the longest x1 25.6 us: shards(): jnp.einsum('gkpt,akt->gpa', built, columns, preferred_element_type=jnp.fl...]
    scatter x2 -> x0, local copies, waits for them, and re-layouts: 27.4 us -> none  [the longest x1 18.7 us: bucket_tiles(): jnp.full((n_dest, slots), -1, jnp.int32).at[target, place].set(labels)]
    all_to_all x1 -> x0, blocking collectives: 20.2 us -> none  [shards(): lax.all_to_all(buffer, 'col', split_axis=0, concat_axis=0, tiled=True)]
    all_gather x1 -> x0, blocking collectives: 14.5 us -> none  [shards(): piece_marks = lax.all_gather(got_marks[None], 'row', axis=0, tiled=True)]
    all_to_all x1 -> x0, starting transfers between devices: 7.58 us -> none  [shards(): lax.all_to_all(marks, 'col', split_axis=0, concat_axis=0, tiled=True)]
    all_gather x1 -> x0, waiting for transfers between devices: 7.3 us -> none  [shards(): piece_tiles = lax.all_gather(got_tiles[None], 'row', axis=0, tiled=True)]
  transfers between devices with their start and end apart: 3 -> 0, of which waited for: 3 -> 0; matrix products, arithmetic and copies ran while one was open for 9% -> 0% of each run, Pallas kernels for 0% -> 0%
where the time goes in v1:
time: 120 us; the launch traced here: 119 us
  Pallas kernels  112 us (93%)
  other arithmetic  5.19 us (4%)
  local copies, waits for them, and re-layouts  2.58 us (2%)
    pallas_call x1, Pallas kernels, ladder(): pl.pallas_call(ladder_kernel, out_shape=jax.ShapeDtypeStruct((128, ab), f...  109 us

profile of v1, /device:TPU:22, one launch (start us, length us, event | category | flops | bytes accessed | tf_op | source)
XLA Modules:
  0.0 119.4 jit_solution(5100658502186757867)
XLA Ops:
  0.0 0.7 fusion.5
  0.7 0.8 fusion
  1.5 0.7 and_select_fusion.1
  2.1 0.9 convert_reduce_fusion.1
  3.0 1.3 %multiply_add_fusion.place_ref = s32[128]{0:T(128)} fusion(s32[128]{0:T(128)S(1)} %convert_reduce_fusion.1, s32[1,128]{1,0:T(1,128)} %param.4), kind=kLoop, calls=%fused_computation.23 | loop fusion | flops 2176 | bytes 1536 | tf_op jit(solution)/shard_map/add | solution.py:496
  4.3 0.9 convert_reduce_fusion
  5.2 0.1 select_n.39
  5.3 0.6 pad.4.inv_ref
  5.9 2.3 %bucket.1.buf_ref = bf16[256,16,128]{2,1,0:T(8,128)(2,1)} custom-call(s32[128]{0:T(128)} %multiply_add_fusion.place_ref, bf16[128,16,128]{2,1,0:T(8,128)(2,1)} %bitcast.7), custom_call_target="tpu_custom_call" | custom-call | tf_op jit(solution)/shard_map/bucket/pallas_call | solution.py:28
  8.2 109.3 %ladder.1 = f32[128,1024]{1,0:T(8,128)} custom-call(bf16[256,16,128]{2,1,0:T(8,128)(2,1)} %bucket.1.buf_ref, s32[16,1,128]{2,1,0:T(1,128)} %pad.4.inv_ref, bf16[1024,4096]{1,0:T(8,128)(2,1)} %int_ref.1), custom_call_target="tpu_custom_call" | custom-call | tf_op jit(solution)/shard_map/ladder/pallas_call | solution.py:482
  117.5 1.9 %copy.5 = f32[128,1024]{1,0:T(8,128)} copy(f32[128,1024]{1,0:T(8,128)} %ladder.1) | data formatting | bytes 1048576
  (2 shorter events, 0.0 us)

commit v2 on v1

--- a/solution.py
+++ b/solution.py
@@ -16,25 +16,49 @@
 OFFSET = {OWN: 0, PART: 0, ZM: 3, PZM: 3, ZP: 1, PZP: 1, Z2: 2, PZ2: 2}
 
 
-def bucket_kernel(place_ref, lam_ref, out_ref):
+def bucket_kernel(ids_ref, lam_ref, out_ref, inv_ref, used):
+    n_col, _, _ = inv_ref.shape
+    kt = 32
+    first = lax.axis_index("col") * CAP
+
+    def clear(b, carry):
+        used[b] = 0
+        for k in range(kt):
+            inv_ref[b, 0, k] = n_col * CAP
+        return carry
+
+    lax.fori_loop(0, n_col, clear, 0)
+
     def body(s, carry):
-        out_ref[place_ref[s]] = lam_ref[s]
+        tile = ids_ref[0, s]
+        b = tile // kt
+        slot = used[b]
+        used[b] = slot + 1
+        inv_ref[b, 0, tile % kt] = first + slot
+        out_ref[b * CAP + slot] = lam_ref[s]
         return carry
 
     lax.fori_loop(0, lam_ref.shape[0], body, 0, unroll=8)
 
 
-def bucket(place, tiles, slots):
+def bucket(ids, tiles, n_col):
     return pl.pallas_call(
         bucket_kernel,
-        out_shape=jax.ShapeDtypeStruct((slots,) + tiles.shape[1:], tiles.dtype),
+        out_shape=(
+            jax.ShapeDtypeStruct((n_col * CAP,) + tiles.shape[1:], tiles.dtype),
+            jax.ShapeDtypeStruct((n_col, 1, 128), jnp.int32),
+        ),
         in_specs=[
             pl.BlockSpec(memory_space=pltpu.SMEM),
             pl.BlockSpec(memory_space=pltpu.VMEM),
         ],
-        out_specs=pl.BlockSpec(memory_space=pltpu.VMEM),
+        out_specs=(
+            pl.BlockSpec(memory_space=pltpu.VMEM),
+            pl.BlockSpec(memory_space=pltpu.SMEM),
+        ),
+        scratch_shapes=[pltpu.SMEM((n_col,), jnp.int32)],
         name="bucket",
-    )(place, tiles)
+    )(ids, tiles)
 
 
 def wide(scale, width):
@@ -83,16 +107,19 @@
 
 def ladder_kernel(
     buf_ref, inv_ref, int_ref, out_ref,
-    r0, r1, r2, r3, r4, r5, r6, r7, tabs, smem, ints, dense, prod,
+    r0, r1, r2, r3, r4, r5, r6, r7, tabs, smem, ints, dense0, dense1, prod,
     q1, s1, q2, s2, q3, s3, q4, s4,
     rq1, rs1, rq2, rs2, rq3, rs3, rq4, rs4,
+    q5, s5, rq5, rs5, acc5, q6, s6,
     acc1, acc2, fin1, fin2,
     int_sem, smem_sem, loc_sem,
     ta_send, ta_recv, t_send, t_recv,
     a_send, a_recv, b_send, b_recv, c_send, c_recv, d_send, d_recv,
     q1_send, q1_recv, q2_send, q2_recv, q3_send, q3_recv, q4_send, q4_recv,
+    e_recv, e_send, q5_send, q5_recv, s5_send, s5_recv, q6_send, s6_send,
     s1_send, s1_recv, s2_send, s2_recv, s3_send, s3_recv, s4_send, s4_recv,
 ):
+    dense = (dense0, dense1)
     rbuf = (r0, r1, r2, r3, r4, r5, r6, r7)
     row, col = lax.axis_index("row"), lax.axis_index("col")
     z, core = row // 2, row % 2
@@ -135,12 +162,13 @@
     lax.fori_loop(1, 16, send_table, 0)
 
     here = pl.ds(pl.multiple_of(col * CAP, CAP), CAP)
-    pltpu.make_async_copy(buf_ref.at[here], r0.at[here], a_recv.at[0]).start()
+    pltpu.make_async_copy(buf_ref.at[here], r0.at[here], e_recv.at[0]).start()
 
     def tile_copy(dy, j):
         to = ((y + 4 - dy) % 4) * 4 + (x + j) % 4
         there = pl.ds(pl.multiple_of(to * CAP, CAP), CAP)
-        return remote(buf_ref.at[there], r0.at[here], a_send.at[dy * 4 + j], a_recv.at[dy], row, to)
+        arrival = e_recv.at[j] if dy == 0 else a_recv.at[dy]
+        return remote(buf_ref.at[there], r0.at[here], a_send.at[dy * 4 + j], arrival, row, to)
 
     for dy in DYS:
         for j in range(1 if dy == 0 else 0, 4):
@@ -151,14 +179,11 @@
     for r in rbuf:
         r[16 * CAP] = zero
 
-    wait_bytes(tabs.at[OWN], ta_recv)
     t_own = [
         remote(tabs.at[OWN], tabs.at[ZM], t_send.at[0], t_recv.at[ZM], up, col),
         remote(tabs.at[OWN], tabs.at[ZP], t_send.at[1], t_recv.at[ZP], down, col),
         remote(tabs.at[OWN], tabs.at[PART], t_send.at[2], t_recv.at[PART], partner, col),
     ]
-    for t in t_own:
-        t.start()
 
     def quarter(dy):
         return pl.ds(pl.multiple_of(((y + dy) % 4) * 4 * CAP, 4 * CAP), 4 * CAP)
@@ -182,10 +207,46 @@
         src, dst = ((ZM, PZM), (ZP, PZP), (Z2, PZ2))[which]
         return remote(rbuf[src].at[at], rbuf[dst].at[at], d_send.at[which, dy], d_recv.at[which, dy], partner, col)
 
-    for dy in DYS:
+    def e_copies(j):
+        at = pl.ds(pl.multiple_of((y * 4 + (x + 4 - j) % 4) * CAP, CAP), CAP)
+        return [
+            remote(r0.at[at], rbuf[ZM].at[at], e_send.at[0, j], b_recv.at[0, 0], up, col),
+            remote(r0.at[at], rbuf[ZP].at[at], e_send.at[1, j], b_recv.at[1, 0], down, col),
+            remote(r0.at[at], rbuf[PART].at[at], e_send.at[2, j], b_recv.at[2, 0], partner, col),
+        ]
+
+    def fetch(step):
+        return pltpu.make_async_copy(tabs.at[step], smem.at[step], smem_sem.at[step])
+
+    def build(step, into, g):
+        tiles = rbuf[step]
+        for k in range(32):
+            dense[into][pl.ds(pl.multiple_of(g * 16, 16), 16), k * 128 : (k + 1) * 128] = tiles[smem[step, g, 0, k]]
+
+    def build_all(step, into, first=0, count=16):
+        def body(g, carry):
+            build(step, into, first + g)
+            return carry
+
+        lax.fori_loop(0, count, body, 0)
+
+    for j in range(4):
+        at = pl.ds(pl.multiple_of((y * 4 + (x + 4 - j) % 4) * CAP, CAP), CAP)
+        wait_bytes(r0.at[at], e_recv.at[j])
+        for copy in e_copies(j):
+            copy.start()
+        if j == 0:
+            wait_bytes(tabs.at[OWN], ta_recv)
+            for t in t_own:
+                t.start()
+            fetch(OWN).start()
+    for dy in DYS[1:]:
         wait_bytes(r0.at[quarter(dy)], a_recv.at[dy])
         for copy in b_copies(dy):
             copy.start()
+        if dy == DYS[1]:
+            fetch(OWN).wait()
+    build_all(OWN, 0)
 
     def arrived(buf, sem, dys=DYS):
         for dy in dys:
@@ -196,25 +257,16 @@
         ki = core if step in (OWN, ZM, ZP, Z2) else 1 - core
         return zi, ki
 
-    def compute(step):
-        fetch = pltpu.make_async_copy(tabs.at[step], smem, smem_sem)
-        fetch.start()
-        fetch.wait()
-        tiles = rbuf[step]
-
-        def build(g, carry):
-            for k in range(32):
-                dense[pl.ds(pl.multiple_of(g * 16, 16), 16), k * 128 : (k + 1) * 128] = tiles[smem[g, 0, k]]
+    def product(at, h, following=None):
+        def columns(n, carry):
+            cols = pl.ds(pl.multiple_of(n * 256, 256), 256)
+            prod[:, cols] = lax.dot_general(dense[at][...], ints[cols, :], NT, preferred_element_type=jnp.float32)
+            if following is not None:
+                for g in range(4):
+                    build(following, 1 - at, n * 4 + g)
             return carry
 
-        lax.fori_loop(0, 16, build, 0)
-
-        def columns(n, carry):
-            at = pl.ds(pl.multiple_of(n * 256, 256), 256)
-            prod[:, at] = lax.dot_general(dense[...], ints[at, :], NT, preferred_element_type=jnp.float32)
-            return carry
-
-        lax.fori_loop(0, 4, columns, 0)
+        lax.fori_loop(2 * h, 2 * h + 2, columns, 0)
 
     def q1_copies(step):
         zi, ki = where_from(step)
@@ -254,6 +306,26 @@
             remote(s4.at[zi], rs4.at[d], s4_send.at[zi], s4_recv.at[d], row, to),
         )
 
+    def q5_copies(step, e):
+        _, ki = where_from(step)
+        xd = 2 * ki + e
+        d = (x + 3 - xd) % 4
+        to = y * 4 + xd
+        at = 0 if step == Z2 else 1
+        return (
+            remote(q5.at[at, e], rq5.at[d], q5_send.at[at, e], q5_recv.at[d], row, to),
+            remote(s5.at[at, e], rs5.at[d], s5_send.at[at, e], s5_recv.at[d], row, to),
+        )
+
+    def q6_copies(step):
+        zi, _ = where_from(step)
+        d = (y + 3 - zi) % 4
+        to = zi * 4 + x
+        return (
+            remote(q6, rq3.at[d], q6_send, q3_recv.at[d], row, to),
+            remote(s6, rs3.at[d], s6_send, s3_recv.at[d], row, to),
+        )
+
     def move(src, dst):
         rows = src.shape[0]
 
@@ -264,9 +336,24 @@
 
         lax.fori_loop(0, rows // 16, body, 0)
 
-    def first_sends(step):
-        zi, ki = where_from(step)
-        left, right = prod.at[:, pl.ds(0, 512)], prod.at[:, pl.ds(512, 512)]
+    def left_sends(step):
+        zi, ki = where_from(step)
+        left = prod.at[:, pl.ds(0, 512)]
+        if step in (Z2, PZ2):
+            for e in range(2):
+                part = left.at[pl.ds(e * 128, 128), :]
+
+                @pl.when(x != 2 * ki + e)
+                def _():
+                    quantize(part, q5.at[0 if step == Z2 else 1, e], s5.at[0 if step == Z2 else 1, e])
+                    for copy in q5_copies(step, e):
+                        copy.start()
+
+                @pl.when(x == 2 * ki + e)
+                def _():
+                    move(part, acc5)
+
+            return
 
         @pl.when(y != zi)
         def _():
@@ -278,6 +365,9 @@
         def _():
             move(left, acc1.at[ki])
 
+    def right_sends(step):
+        zi, ki = where_from(step)
+        right = prod.at[:, pl.ds(512, 512)]
         for e in range(2):
             part = right.at[pl.ds(e * 128, 128), :]
 
@@ -291,8 +381,28 @@
             def _():
                 move(part, acc2.at[zi])
 
-    def second_sends(step):
-        zi, ki = where_from(step)
+    def second_left(step):
+        zi, ki = where_from(step)
+        if step in (Z2, PZ2):
+
+            @pl.when(x // 2 == ki)
+            def _():
+                for d in range(3):
+                    wait_bytes(rq5.at[d], q5_recv.at[d])
+                    wait_bytes(rs5.at[d], s5_recv.at[d])
+                add_coded(acc5, rq5, rs5)
+
+                @pl.when(y != zi)
+                def _():
+                    quantize(acc5, q6, s6)
+                    for copy in q6_copies(step):
+                        copy.start()
+
+                @pl.when(y == zi)
+                def _():
+                    move(acc5, fin1)
+
+            return
 
         @pl.when(y == zi)
         def _():
@@ -313,6 +423,9 @@
                 def _():
                     move(part, fin1)
 
+    def second_right(step):
+        zi, ki = where_from(step)
+
         @pl.when(x // 2 == ki)
         def _():
             for d in range(3):
@@ -330,9 +443,18 @@
             def _():
                 move(acc2.at[zi], fin2)
 
+    def run(step, at, following=None):
+        product(at, 0, following)
+        left_sends(step)
+        product(at, 1, following)
+        right_sends(step)
+
+    def second(step):
+        second_left(step)
+        second_right(step)
+
     load.wait()
-    compute(OWN)
-    first_sends(OWN)
+    run(OWN, 0)
 
     wait_bytes(tabs.at[ZM], t_recv.at[ZM])
     wait_bytes(tabs.at[ZP], t_recv.at[ZP])
@@ -343,6 +465,9 @@
     ]
     for t in t_more:
         t.start()
+    wait_bytes(tabs.at[PART], t_recv.at[PART])
+    for step in (PART, ZM, ZP):
+        fetch(step).start()
 
     def pass_on(dys):
         for dy in dys:
@@ -352,55 +477,53 @@
             d_copy(0, dy).start()
             d_copy(1, dy).start()
 
-    pass_on(DYS[:2])
-    wait_bytes(tabs.at[PART], t_recv.at[PART])
-    arrived(PART, b_recv.at[2])
-    compute(PART)
-    first_sends(PART)
-    second_sends(OWN)
-    pass_on(DYS[2:])
-
-    compute(ZM)
-    first_sends(ZM)
-    second_sends(PART)
-
-    wait_bytes(tabs.at[Z2], t_recv.at[Z2])
-    t_last = remote(tabs.at[Z2], tabs.at[PZ2], t_send.at[6], t_recv.at[PZ2], partner, col)
-    t_last.start()
-
-    compute(ZP)
-    first_sends(ZP)
-    second_sends(ZM)
-
     def pass_far(dys):
         for dy in dys:
             wait_bytes(rbuf[Z2].at[quarter(dy)], c_recv.at[dy])
             d_copy(2, dy).start()
 
+    pass_on(DYS[:1])
+    arrived(PART, b_recv.at[2])
+    for step in (PART, ZM, ZP):
+        fetch(step).wait()
+    build_all(PART, 1)
+    run(PART, 1)
+    pass_on(DYS[1:])
+
+    build_all(ZM, 0)
+    run(ZM, 0, ZP)
     wait_bytes(tabs.at[PZM], t_recv.at[PZM])
+    wait_bytes(tabs.at[PZP], t_recv.at[PZP])
+    wait_bytes(tabs.at[Z2], t_recv.at[Z2])
+    t_last = remote(tabs.at[Z2], tabs.at[PZ2], t_send.at[6], t_recv.at[PZ2], partner, col)
+    t_last.start()
+    for step in (PZM, PZP, Z2):
+        fetch(step).start()
     arrived(PZM, d_recv.at[0])
-    compute(PZM)
-    first_sends(PZM)
-    second_sends(ZP)
-    pass_far(DYS[:2])
-
-    wait_bytes(tabs.at[PZP], t_recv.at[PZP])
+    for step in (PZM, PZP, Z2):
+        fetch(step).wait()
+
+    run(ZP, 1, PZM)
+    second(OWN)
     arrived(PZP, d_recv.at[1])
-    compute(PZP)
-    first_sends(PZP)
-    second_sends(PZM)
-    pass_far(DYS[2:])
-
-    compute(Z2)
-    first_sends(Z2)
-    second_sends(PZP)
-
+    run(PZM, 0, PZP)
+    second(PART)
+    pass_far(DYS)
+    run(PZP, 1, Z2)
     wait_bytes(tabs.at[PZ2], t_recv.at[PZ2])
+    fetch(PZ2).start()
+    second(ZM)
     arrived(PZ2, d_recv.at[2])
-    compute(PZ2)
-    first_sends(PZ2)
-    second_sends(Z2)
-    second_sends(PZ2)
+    fetch(PZ2).wait()
+    run(Z2, 0, PZ2)
+    second(ZP)
+    second(PZM)
+    run(PZ2, 1)
+    second(PZP)
+    second_left(Z2)
+    second_left(PZ2)
+    second_right(Z2)
+    second_right(PZ2)
 
     for d in range(3):
         wait_bytes(rq3.at[d], q3_recv.at[d])
@@ -421,7 +544,7 @@
     for dy in DYS:
         for j in range(1 if dy == 0 else 0, 4):
             tile_copy(dy, j).wait_send()
-        for copy in b_copies(dy):
+        for copy in sum((e_copies(j) for j in range(4)), []) if dy == 0 else b_copies(dy):
             copy.wait_send()
         c_copy(dy).wait_send()
         for which in range(3):
@@ -429,10 +552,12 @@
     for step in STEPS:
         zi, ki = where_from(step)
 
-        @pl.when(y != zi)
-        def _():
-            for copy in q1_copies(step):
-                copy.wait_send()
+        if step not in (Z2, PZ2):
+
+            @pl.when(y != zi)
+            def _():
+                for copy in q1_copies(step):
+                    copy.wait_send()
 
         for e in range(2):
 
@@ -440,16 +565,24 @@
             def _():
                 for copy in q2_copies(step, e):
                     copy.wait_send()
-
-            @pl.when((y == zi) & (x != 2 * ki + e))
-            def _():
-                for copy in q3_copies(step, e):
-                    copy.wait_send()
+                if step in (Z2, PZ2):
+                    for copy in q5_copies(step, e):
+                        copy.wait_send()
+
+            if step not in (Z2, PZ2):
+
+                @pl.when((y == zi) & (x != 2 * ki + e))
+                def _():
+                    for copy in q3_copies(step, e):
+                        copy.wait_send()
 
         @pl.when((y != zi) & (x // 2 == ki))
         def _():
             for copy in q4_copies(step):
                 copy.wait_send()
+            if step in (Z2, PZ2):
+                for copy in q6_copies(step):
+                    copy.wait_send()
 
 
 def ladder(buf, inv, integrals):
@@ -460,8 +593,8 @@
     vmem = pltpu.VMEM
     scratch = [vmem((16 * CAP + 1, 16, 128), bf16) for _ in range(8)]
     scratch += [
-        vmem((8, 16, 1, 128), jnp.int32), pltpu.SMEM((16, 1, 128), jnp.int32),
-        vmem((ab, cd), bf16), vmem((256, cd), bf16), vmem((256, ab), f32),
+        vmem((8, 16, 1, 128), jnp.int32), pltpu.SMEM((8, 16, 1, 128), jnp.int32),
+        vmem((ab, cd), bf16), vmem((256, cd), bf16), vmem((256, cd), bf16), vmem((256, ab), f32),
         vmem((8, 256, half), i16), vmem((8, 8, 128), f32),
         vmem((8, 2, 128, half), i16), vmem((8, 2, 8, 128), f32),
         vmem((2, 2, 128, half), i16), vmem((2, 2, 8, 128), f32),
@@ -470,12 +603,15 @@
         vmem((4, 3, 128, half), i16), vmem((4, 3, 8, 128), f32),
         vmem((3, 128, half), i16), vmem((3, 8, 128), f32),
         vmem((3, 128, half), i16), vmem((3, 8, 128), f32),
+        vmem((2, 2, 128, half), i16), vmem((2, 2, 8, 128), f32), vmem((3, 128, half), i16), vmem((3, 8, 128), f32),
+        vmem((128, half), f32), vmem((128, half), i16), vmem((8, 128), f32),
         vmem((2, 256, half), f32), vmem((4, 128, half), f32),
         vmem((128, half), f32), vmem((128, half), f32),
-        dma, dma, dma,
+        dma, dma((8,)), dma,
         dma((16,)), dma, dma((7,)), dma((8,)),
         dma((16,)), dma((4,)), dma((3, 4)), dma((3, 4)), dma((4,)), dma((4,)), dma((3, 4)), dma((3, 4)),
         dma((8,)), dma((2, 3)), dma((8, 2)), dma((4, 3)), dma((2, 2)), dma((3,)), dma((4,)), dma((3,)),
+        dma((4,)), dma((3, 4)), dma((2, 2)), dma((3,)), dma((2, 2)), dma((3,)), dma, dma,
         dma((8,)), dma((2, 3)), dma((8, 2)), dma((4, 3)), dma((2, 2)), dma((3,)), dma((4,)), dma((3,)),
     ]
     any_space = pl.BlockSpec(memory_space=pl.ANY)
@@ -490,24 +626,9 @@
     )(buf, inv, integrals)
 
 
-def tables(ids, col, n_col, kt_dev):
-    block = ids // kt_dev
-    lower = (block[:, None] == block[None, :]) & (ids[None, :] < ids[:, None])
-    place = block * CAP + jnp.sum(lower.astype(jnp.int32), axis=1)
-    tile = jnp.arange(n_col * kt_dev, dtype=jnp.int32)
-    present = jnp.any(ids[None, :] == tile[:, None], axis=1)
-    before = (block[None, :] == (tile // kt_dev)[:, None]) & (ids[None, :] < tile[:, None])
-    rank = jnp.sum(before.astype(jnp.int32), axis=1)
-    inv = jnp.where(present, col * CAP + rank, n_col * CAP).reshape(n_col, 1, kt_dev)
-    return place, jnp.pad(inv, ((0, 0), (0, 0), (0, 128 - kt_dev)))
-
-
 def shards(lam_tiles, lam_ids, integrals):
-    n_col = lax.axis_size("col")
     _, s_count, pairs, tile = lam_tiles.shape
-    kt_dev = integrals.shape[1] // tile
-    place, inv = tables(lam_ids.reshape(-1), lax.axis_index("col"), n_col, kt_dev)
-    buf = bucket(place, lam_tiles.reshape(s_count, pairs, tile), n_col * CAP)
+    buf, inv = bucket(lam_ids, lam_tiles.reshape(s_count, pairs, tile), lax.axis_size("col"))
     return ladder(buf, inv, integrals)
 
 

time: 120 us -> 92.7 us (0.77)
  the two profiles are of different devices: /device:TPU:22 before, /device:TPU:65 now
where the time goes in v2:
time: 92.7 us; the launch traced here: 92.5 us
  Pallas kernels  90.6 us (98%)
  local copies, waits for them, and re-layouts  1.89 us (2%)
    pallas_call x1, Pallas kernels, ladder(): pl.pallas_call(ladder_kernel, out_shape=jax.ShapeDtypeStruct((128, ab), f...  86.9 us
    pallas_call x1, Pallas kernels, bucket(): pl.pallas_call(bucket_kernel, out_shape=(jax.ShapeDtypeStruct((n_col * CA...  3.76 us
    unnamed x1, local copies, waits for them, and re-layouts  1.89 us

profile of v2, /device:TPU:65, one launch (start us, length us, event | category | flops | bytes accessed | tf_op | source)
XLA Modules:
  0.0 92.5 jit_solution(215515094905157418)
XLA Ops:
  0.0 3.8 %bucket.1 = (bf16[256,16,128]{2,1,0:T(8,128)(2,1)}, s32[16,1,128]{2,1,0:T(1,128)}) custom-call(s32[1,128]{1,0:T(1,128)} %ids_ref.1, bf16[128,16,128]{2,1,0:T(8,128)(2,1)} %bitcast.1), custom_call_target="tpu_custom_call" | custom-call | tf_op jit(solution)/shard_map/bucket/pallas_call | solution.py:45
  3.8 86.9 %ladder.1 = f32[128,1024]{1,0:T(8,128)} custom-call(bf16[256,16,128]{2,1,0:T(8,128)(2,1)} %get-tuple-element.7.buf_ref, s32[16,1,128]{2,1,0:T(1,128)} %get-tuple-element.8.inv_ref, bf16[1024,4096]{1,0:T(8,128)(2,1)} %int_ref.1), custom_call_target="tpu_custom_call" | custom-call | tf_op jit(solution)/shard_map/ladder/pallas_call | solution.py:618
  90.6 1.9 %copy.5 = f32[128,1024]{1,0:T(8,128)} copy(f32[128,1024]{1,0:T(8,128)} %ladder.1) | data formatting | bytes 1048576

commit v3 on v2

v3 whole, which is shorter than its diff:
```python
import functools

import jax
import jax.numpy as jnp
from jax import lax
from jax.experimental import pallas as pl
from jax.experimental.pallas import tpu as pltpu
from jax.sharding import PartitionSpec as P

CAP = 16
MESH = pl.DeviceIdType.MESH
DYS = (0, 1, 3, 2)
NT = (((1,), (1,)), ((), ()))
OWN, PART, A, B, PA, PB, Z2, PZ2 = range(8)
STEPS = (OWN, PART, A, PA, B, PB, Z2, PZ2)
Y_FIRST = {"L": (OWN, PART, A, PA, B, PB), "M": (OWN, PART, A, PA), "N": ()}
GROUP_REFS = (
    "q", "s", "rq", "rs", "acc", "q4", "s4", "rf", "rsf", "fin",
    "q_sem", "s_sem", "rq_sem", "rs_sem", "q4_sem", "s4_sem", "rf_sem", "rsf_sem",
)
Y_REFS = (
    "q1", "s1", "q3", "s3", "rq1", "rs1", "acc1",
    "q1_sem", "s1_sem", "rq1_sem", "rs1_sem", "q3_sem", "s3_sem",
)
GROUPS = {"L": (0, 256), "M": (256, 256), "N": (512, 512)}


def bucket_kernel(ids_ref, lam_ref, out_ref, inv_ref, used):
    n_col, _, _ = inv_ref.shape
    kt = 32
    first = lax.axis_index("col") * CAP

    def clear(b, carry):
        used[b] = 0
        for k in range(kt):
            inv_ref[b, 0, k] = n_col * CAP
        return carry

    lax.fori_loop(0, n_col, clear, 0)

    def body(s, carry):
        tile = ids_ref[0, s]
        b = tile // kt
        slot = used[b]
        used[b] = slot + 1
        inv_ref[b, 0, tile % kt] = first + slot
        out_ref[b * CAP + slot] = lam_ref[s]
        return carry

    lax.fori_loop(0, lam_ref.shape[0], body, 0, unroll=8)


def bucket(ids, tiles, n_col):
    return pl.pallas_call(
        bucket_kernel,
        out_shape=(
            jax.ShapeDtypeStruct((n_col * CAP,) + tiles.shape[1:], tiles.dtype),
            jax.ShapeDtypeStruct((n_col, 1, 128), jnp.int32),
        ),
        in_specs=[
            pl.BlockSpec(memory_space=pltpu.SMEM),
            pl.BlockSpec(memory_space=pltpu.VMEM),
        ],
        out_specs=(
            pl.BlockSpec(memory_space=pltpu.VMEM),
            pl.BlockSpec(memory_space=pltpu.SMEM),
        ),
        scratch_shapes=[pltpu.SMEM((n_col,), jnp.int32)],
        name="bucket",
    )(ids, tiles)


def wide(scale, width):
    return jnp.concatenate([jnp.concatenate([scale, scale], axis=0)] * (width // 128), axis=1)


def quantize(src, dst, scale_dst):
    rows, width = src.shape

    def largest(r, m):
        a = jnp.abs(src[pl.ds(r * 16, 16), :])
        for j in range(width // 128):
            part = a[:, j * 128 : (j + 1) * 128]
            m = jnp.maximum(m, jnp.maximum(part[:8], part[8:]))
        return m

    m = lax.fori_loop(0, rows // 16, largest, jnp.zeros((8, 128), jnp.float32), unroll=2)
    scale_dst[...] = m * (1.0 / 32767.0)
    inverse = wide(jnp.where(m > 0.0, 32767.0 / m, 0.0), width)

    def code(r, carry):
        at = pl.ds(pl.multiple_of(r * 16, 16), 16)
        dst[at, :] = jnp.round(src[at, :] * inverse).astype(jnp.int32).astype(jnp.int16)
        return carry

    lax.fori_loop(0, rows // 16, code, 0, unroll=2)


def add_coded(acc, coded, scales, factor=None, out=None):
    rows, width = acc.shape
    w = [wide(scales[j], width) for j in range(3)]

    def body(r, carry):
        at = pl.ds(pl.multiple_of(r * 16, 16), 16)
        total = acc[at, :]
        for j in range(3):
            total = total + coded[j, at, :].astype(jnp.int32).astype(jnp.float32) * w[j]
        if out is None:
            acc[at, :] = total
        else:
            out[at, :] = factor * total
        return carry

    lax.fori_loop(0, rows // 16, body, 0, unroll=2)


def ladder_kernel(
    buf_ref, inv_ref, int_ref, out_ref,
    r0, r1, r2, r3, r4, r5, r6, r7, tabs, smem, ints, dense0, dense1, prod,
    int_sem, smem_sem, e_recv, e_send,
    ta_send, ta_recv, t_send, t_recv,
    a_send, a_recv, b_send, b_recv, c_send, c_recv, d_send, d_recv,
    *by_group
):
    refs = {g: dict(zip(GROUP_REFS, by_group[i * len(GROUP_REFS) :])) for i, g in enumerate(GROUPS)}
    for i, g in enumerate("LM"):
        refs[g].update(zip(Y_REFS, by_group[len(GROUPS) * len(GROUP_REFS) + i * len(Y_REFS) :]))
    dense = (dense0, dense1)
    rbuf = (r0, r1, r2, r3, r4, r5, r6, r7)
    row, col = lax.axis_index("row"), lax.axis_index("col")
    z, core = row // 2, row % 2
    y, x = col // 4, col % 4
    up = ((z + 1) % 4) * 2 + core
    down = ((z + 3) % 4) * 2 + core
    partner = z * 2 + (1 - core)
    first_row = jnp.where(core == 0, up, down)
    second_row = jnp.where(core == 0, down, up)

    barrier = pltpu.get_barrier_semaphore()

    def greet(j, carry):
        pl.semaphore_signal(barrier, inc=1, device_id={"row": row, "col": (col + j) % 16}, device_id_type=MESH)
        return carry

    lax.fori_loop(1, 16, greet, 0)
    for other in (up, down, partner):
        pl.semaphore_signal(barrier, inc=1, device_id={"row": other, "col": col}, device_id_type=MESH)
    pl.semaphore_wait(barrier, 18)

    def remote(src, dst, send, recv, to_row, to_col):
        return pltpu.make_async_remote_copy(
            src_ref=src, dst_ref=dst, send_sem=send, recv_sem=recv,
            device_id={"row": to_row, "col": to_col}, device_id_type=MESH,
        )

    def wait_bytes(ref, sem):
        pltpu.make_async_copy(ref, ref, sem).wait()

    load = pltpu.make_async_copy(int_ref, ints, int_sem)

    mine = pl.ds(col, 1)
    own_table = pltpu.make_async_copy(inv_ref.at[mine], tabs.at[OWN, mine], ta_recv)
    own_table.start()

    def send_table(j, carry):
        to = (col + j) % 16
        remote(inv_ref.at[pl.ds(to, 1)], tabs.at[OWN, mine], ta_send.at[j], ta_recv, row, to).start()
        return carry

    lax.fori_loop(1, 16, send_table, 0)

    here = pl.ds(pl.multiple_of(col * CAP, CAP), CAP)
    pltpu.make_async_copy(buf_ref.at[here], r0.at[here], e_recv.at[0]).start()

    def tile_copy(dy, j):
        to = ((y + 4 - dy) % 4) * 4 + (x + j) % 4
        there = pl.ds(pl.multiple_of(to * CAP, CAP), CAP)
        arrival = e_recv.at[j] if dy == 0 else a_recv.at[dy]
        return remote(buf_ref.at[there], r0.at[here], a_send.at[dy * 4 + j], arrival, row, to)

    for dy in DYS:
        for j in range(1 if dy == 0 else 0, 4):
            tile_copy(dy, j).start()
    load.start()

    zero = jnp.zeros((16, 128), jnp.bfloat16)
    for r in rbuf:
        r[16 * CAP] = zero

    t_own = [
        remote(tabs.at[OWN], tabs.at[A], t_send.at[0], t_recv.at[A], first_row, col),
        remote(tabs.at[OWN], tabs.at[B], t_send.at[1], t_recv.at[B], second_row, col),
        remote(tabs.at[OWN], tabs.at[PART], t_send.at[2], t_recv.at[PART], partner, col),
    ]

    def quarter(dy):
        return pl.ds(pl.multiple_of(((y + dy) % 4) * 4 * CAP, 4 * CAP), 4 * CAP)

    def b_copies(dy, which):
        at = quarter(dy)
        to, buf = ((first_row, A), (second_row, B), (partner, PART))[which]
        return remote(r0.at[at], rbuf[buf].at[at], b_send.at[which, dy], b_recv.at[which, dy], to, col)

    def c_copy(dy):
        at = quarter(dy)
        return remote(rbuf[A].at[at], rbuf[Z2].at[at], c_send.at[dy], c_recv.at[dy], first_row, col)

    def d_copy(which, dy):
        at = quarter(dy)
        src, dst = ((A, PA), (B, PB), (Z2, PZ2))[which]
        return remote(rbuf[src].at[at], rbuf[dst].at[at], d_send.at[which, dy], d_recv.at[which, dy], partner, col)

    def block(j):
        return pl.ds(pl.multiple_of((y * 4 + (x + 4 - j) % 4) * CAP, CAP), CAP)

    def e_copy(j, which):
        at = block(j)
        to, buf = ((first_row, A), (second_row, B), (partner, PART))[which]
        return remote(r0.at[at], rbuf[buf].at[at], e_send.at[which, j], b_recv.at[which, 0], to, col)

    def fetch(step):
        return pltpu.make_async_copy(tabs.at[step], smem.at[step], smem_sem.at[step])

    def build(step, into, g):
        tiles = rbuf[step]
        for k in range(32):
            dense[into][pl.ds(pl.multiple_of(g * 16, 16), 16), k * 128 : (k + 1) * 128] = tiles[smem[step, g, 0, k]]

    def build_all(step, into, first=0, count=16):
        def body(g, carry):
            build(step, into, first + g)
            return carry

        lax.fori_loop(0, count, body, 0)

    for j in range(4):
        wait_bytes(r0.at[block(j)], e_recv.at[j])
        e_copy(j, 0).start()
        e_copy(j, 2).start()
        if j == 0:
            wait_bytes(tabs.at[OWN], ta_recv)
            for t in t_own:
                t.start()
            fetch(OWN).start()
    for dy in DYS[1:]:
        wait_bytes(r0.at[quarter(dy)], a_recv.at[dy])
        b_copies(dy, 0).start()
        b_copies(dy, 2).start()
        if dy == DYS[1]:
            fetch(OWN).wait()

    def to_second():
        for j in range(4):
            e_copy(j, 1).start()
        for dy in DYS[1:]:
            b_copies(dy, 1).start()

    pl.when(core == 0)(to_second)
    build_all(OWN, 0)

    def arrived(buf, sem, dys=DYS):
        for dy in dys:
            wait_bytes(rbuf[buf].at[quarter(dy)], sem.at[dy])

    def where_from(step):
        ahead, behind = jnp.where(core == 0, 3, 1), jnp.where(core == 0, 1, 3)
        offset = {OWN: 0, PART: 0, A: ahead, PB: ahead, B: behind, PA: behind, Z2: 2, PZ2: 2}[step]
        return (z + offset) % 4, core if step in (OWN, A, B, Z2) else 1 - core

    def product(at, h):
        cols = pl.ds(512 * h, 512)
        prod[:, cols] = lax.dot_general(dense[at][...], ints[cols, :], NT, preferred_element_type=jnp.float32)

    def q1_copies(step, group):
        zi, ki = where_from(step)
        d = (y + 3 - zi) % 4
        r, to = refs[group], zi * 4 + x
        return (
            remote(r["q1"].at[step], r["rq1"].at[ki, d], r["q1_sem"].at[step], r["rq1_sem"].at[ki, d], row, to),
            remote(r["s1"].at[step], r["rs1"].at[ki, d], r["s1_sem"].at[step], r["rs1_sem"].at[ki, d], row, to),
        )

    def place_of(step, group):
        return (int(step == PZ2), 0) if group == "L" else (step, where_from(step)[0])

    def x_copies(step, group, e):
        _, ki = where_from(step)
        d = (x + 3 - (2 * ki + e)) % 4
        r, (at, slot), to = refs[group], place_of(step, group), y * 4 + 2 * ki + e
        return (
            remote(r["q"].at[at, e], r["rq"].at[slot, d], r["q_sem"].at[at, e], r["rq_sem"].at[slot, d], row, to),
            remote(r["s"].at[at, e], r["rs"].at[slot, d], r["s_sem"].at[at, e], r["rs_sem"].at[slot, d], row, to),
        )

    def q3_copies(step, group, e):
        zi, ki = where_from(step)
        xd = 2 * ki + e
        d = (x + 3 - xd) % 4
        r, to = refs[group], zi * 4 + xd
        return (
            remote(r["q3"].at[ki, e], r["rf"].at[d], r["q3_sem"].at[ki, e], r["rf_sem"].at[d], row, to),
            remote(r["s3"].at[ki, e], r["rsf"].at[d], r["s3_sem"].at[ki, e], r["rsf_sem"].at[d], row, to),
        )

    def y_copies(step, group):
        zi, _ = where_from(step)
        d = (y + 3 - zi) % 4
        r, (_, slot), to = refs[group], place_of(step, group), zi * 4 + x
        return (
            remote(r["q4"].at[slot], r["rf"].at[d], r["q4_sem"].at[slot], r["rf_sem"].at[d], row, to),
            remote(r["s4"].at[slot], r["rsf"].at[d], r["s4_sem"].at[slot], r["rsf_sem"].at[d], row, to),
        )

    def move(src, dst):
        rows = src.shape[0]

        def body(r, carry):
            at = pl.ds(pl.multiple_of(r * 16, 16), 16)
            dst[at, :] = src[at, :]
            return carry

        lax.fori_loop(0, rows // 16, body, 0)

    def x_first(step, group):
        _, ki = where_from(step)
        start, width = GROUPS[group]
        r, (at, slot) = refs[group], place_of(step, group)
        for e in range(2):
            part = prod.at[pl.ds(e * 128, 128), pl.ds(start, width)]

            @pl.when(x != 2 * ki + e)
            def _():
                quantize(part, r["q"].at[at, e], r["s"].at[at, e])
                for copy in x_copies(step, group, e):
                    copy.start()

            @pl.when(x == 2 * ki + e)
            def _():
                move(part, r["acc"].at[slot])

    def y_second(step, group):
        zi, ki = where_from(step)
        r, (_, slot) = refs[group], place_of(step, group)

        @pl.when(x // 2 == ki)
        def _():
            for d in range(3):
                wait_bytes(r["rq"].at[slot, d], r["rq_sem"].at[slot, d])
                wait_bytes(r["rs"].at[slot, d], r["rs_sem"].at[slot, d])

            @pl.when(y != zi)
            def _():
                add_coded(r["acc"].at[slot], r["rq"].at[slot], r["rs"].at[slot])
                quantize(r["acc"].at[slot], r["q4"].at[slot], r["s4"].at[slot])
                for copy in y_copies(step, group):
                    copy.start()

            @pl.when(y == zi)
            def _():
                add_coded(r["acc"].at[slot], r["rq"].at[slot], r["rs"].at[slot], 1.0, r["fin"])

    def y_first(step, group):
        zi, ki = where_from(step)
        r, part = refs[group], prod.at[:, pl.ds(*GROUPS[group])]

        @pl.when(y != zi)
        def _():
            quantize(part, r["q1"].at[step], r["s1"].at[step])
            for copy in q1_copies(step, group):
                copy.start()

        @pl.when(y == zi)
        def _():
            move(part, r["acc1"].at[ki])

    def x_second(step, group):
        zi, ki = where_from(step)
        r = refs[group]

        @pl.when(y == zi)
        def _():
            for d in range(3):
                wait_bytes(r["rq1"].at[ki, d], r["rq1_sem"].at[ki, d])
                wait_bytes(r["rs1"].at[ki, d], r["rs1_sem"].at[ki, d])
            add_coded(r["acc1"].at[ki], r["rq1"].at[ki], r["rs1"].at[ki])
            for e in range(2):
                part = r["acc1"].at[ki, pl.ds(e * 128, 128), :]

                @pl.when(x != 2 * ki + e)
                def _():
                    quantize(part, r["q3"].at[ki, e], r["s3"].at[ki, e])
                    for copy in q3_copies(step, group, e):
                        copy.start()

                @pl.when(x == 2 * ki + e)
                def _():
                    move(part, r["fin"])

    def send(step, group):
        (y_first if step in Y_FIRST[group] else x_first)(step, group)

    def pass_sums(step, group):
        (x_second if step in Y_FIRST[group] else y_second)(step, group)

    def run(step, at):
        product(at, 1)
        send(step, "N")
        product(at, 0)
        send(step, "L")
        send(step, "M")

    load.wait()
    run(OWN, 0)

    @pl.when(core == 1)
    def _():
        to_second()

    for step in (A, B, PART):
        wait_bytes(tabs.at[step], t_recv.at[step])
        fetch(step).start()
    t_more = [
        remote(tabs.at[A], tabs.at[Z2], t_send.at[3], t_recv.at[Z2], first_row, col),
        remote(tabs.at[A], tabs.at[PA], t_send.at[4], t_recv.at[PA], partner, col),
        remote(tabs.at[B], tabs.at[PB], t_send.at[5], t_recv.at[PB], partner, col),
    ]
    for t in t_more:
        t.start()

    def pass_on(which, dys=DYS):
        for dy in dys:
            wait_bytes(rbuf[(A, B)[which]].at[quarter(dy)], b_recv.at[which, dy])
            d_copy(which, dy).start()
            if which == 1:
                c_copy(dy).start()

    def pass_far(dys):
        for dy in dys:
            wait_bytes(rbuf[Z2].at[quarter(dy)], c_recv.at[dy])
            d_copy(2, dy).start()

    pass_on(0, DYS[:2])
    arrived(PART, b_recv.at[2])
    for step in (A, B, PART):
        fetch(step).wait()
    build_all(PART, 1)
    run(PART, 1)
    pass_on(0, DYS[2:])
    for step in (PA, PB, Z2):
        wait_bytes(tabs.at[step], t_recv.at[step])
        fetch(step).start()
    t_last = remote(tabs.at[Z2], tabs.at[PZ2], t_send.at[6], t_recv.at[PZ2], partner, col)
    t_last.start()
    build_all(A, 0)
    run(A, 0)
    pass_sums(OWN, "N")
    for step in (PA, PB, Z2):
        fetch(step).wait()
    pass_on(1, DYS[:2])
    arrived(PA, d_recv.at[0])
    build_all(PA, 1)
    run(PA, 1)
    pass_sums(PART, "N")
    pass_on(1, DYS[2:])
    build_all(B, 0)
    run(B, 0)
    pass_sums(OWN, "L")
    pass_sums(OWN, "M")
    pass_sums(A, "N")
    arrived(PB, d_recv.at[1])
    build_all(PB, 1)
    run(PB, 1)
    pass_sums(PART, "L")
    pass_sums(PART, "M")
    pass_sums(PA, "N")
    pass_far(DYS)
    wait_bytes(tabs.at[PZ2], t_recv.at[PZ2])
    fetch(PZ2).start()
    build_all(Z2, 0)
    run(Z2, 0)
    pass_sums(B, "N")
    pass_sums(B, "M")
    pass_sums(A, "L")
    arrived(PZ2, d_recv.at[2])
    fetch(PZ2).wait()
    build_all(PZ2, 1)
    product(1, 1)
    send(PZ2, "N")
    pass_sums(A, "M")
    product(1, 0)
    send(PZ2, "L")
    send(PZ2, "M")
    pass_sums(PA, "L")
    pass_sums(PA, "M")
    pass_sums(PB, "N")
    pass_sums(PB, "M")
    pass_sums(B, "L")
    pass_sums(Z2, "N")
    pass_sums(PB, "L")
    pass_sums(Z2, "L")
    pass_sums(Z2, "M")
    pass_sums(PZ2, "N")
    pass_sums(PZ2, "L")
    pass_sums(PZ2, "M")

    for group in ("N", "L", "M"):
        r, (start, width) = refs[group], GROUPS[group]
        for d in range(3):
            wait_bytes(r["rf"].at[d], r["rf_sem"].at[d])
            wait_bytes(r["rsf"].at[d], r["rsf_sem"].at[d])
        add_coded(r["fin"], r["rf"], r["rsf"], 0.5, out_ref.at[:, pl.ds(start, width)])

    def table_left(j, carry):
        remote(inv_ref.at[mine], tabs.at[OWN, mine], ta_send.at[j], ta_recv, row, (col + j) % 16).wait_send()
        return carry

    lax.fori_loop(1, 16, table_left, 0)
    for t in t_own + t_more + [t_last]:
        t.wait_send()
    for dy in DYS:
        for j in range(1 if dy == 0 else 0, 4):
            tile_copy(dy, j).wait_send()
        for which in range(3):
            for copy in [e_copy(j, which) for j in range(4)] if dy == 0 else [b_copies(dy, which)]:
                copy.wait_send()
        c_copy(dy).wait_send()
        for which in range(3):
            d_copy(which, dy).wait_send()
    for step in STEPS:
        zi, ki = where_from(step)
        y_groups = [g for g in GROUPS if step in Y_FIRST[g]]
        x_groups = [g for g in GROUPS if step not in Y_FIRST[g]]

        @pl.when(y != zi)
        def _():
            for group in y_groups:
                for copy in q1_copies(step, group):
                    copy.wait_send()

        for e in range(2):

            @pl.when((y == zi) & (x != 2 * ki + e))
            def _():
                for group in y_groups:
                    for copy in q3_copies(step, group, e):
                        copy.wait_send()

            @pl.when(x != 2 * ki + e)
            def _():
                for group in x_groups:
                    for copy in x_copies(step, group, e):
                        copy.wait_send()

        @pl.when((y != zi) & (x // 2 == ki))
        def _():
            for group in x_groups:
                for copy in y_copies(step, group):
                    copy.wait_send()


def ladder(buf, inv, integrals):
    ab, cd = integrals.shape
    i16, f32, bf16 = jnp.int16, jnp.float32, jnp.bfloat16
    dma = pltpu.SemaphoreType.DMA
    vmem = pltpu.VMEM
    scratch = [vmem((16 * CAP + 1, 16, 128), bf16) for _ in range(8)]
    scratch += [
        vmem((8, 16, 1, 128), jnp.int32), pltpu.SMEM((8, 16, 1, 128), jnp.int32),
        vmem((ab, cd), bf16), vmem((256, cd), bf16), vmem((256, cd), bf16), vmem((256, ab), f32),
        dma, dma((8,)), dma((4,)), dma((3, 4)),
        dma((16,)), dma, dma((7,)), dma((8,)),
        dma((16,)), dma((4,)), dma((3, 4)), dma((3, 4)), dma((4,)), dma((4,)), dma((3, 4)), dma((3, 4)),
    ]
    for group, (_, width) in GROUPS.items():
        steps, slots = (2, 1) if group == "L" else (8, 4)
        scratch += [
            vmem((steps, 2, 128, width), i16), vmem((steps, 2, 8, 128), f32),
            vmem((slots, 3, 128, width), i16), vmem((slots, 3, 8, 128), f32), vmem((slots, 128, width), f32),
            vmem((slots, 128, width), i16), vmem((slots, 8, 128), f32),
            vmem((3, 128, width), i16), vmem((3, 8, 128), f32), vmem((128, width), f32),
            dma((steps, 2)), dma((steps, 2)), dma((slots, 3)), dma((slots, 3)), dma((slots,)), dma((slots,)), dma((3,)), dma((3,)),
        ]
    for _ in "LM":
        scratch += [
            vmem((8, 256, 256), i16), vmem((8, 8, 128), f32), vmem((2, 2, 128, 256), i16), vmem((2, 2, 8, 128), f32),
            vmem((2, 3, 256, 256), i16), vmem((2, 3, 8, 128), f32), vmem((2, 256, 256), f32),
            dma((8,)), dma((8,)), dma((2, 3)), dma((2, 3)), dma((2, 2)), dma((2, 2)),
        ]
    any_space = pl.BlockSpec(memory_space=pl.ANY)
    return pl.pallas_call(
        ladder_kernel,
        out_shape=jax.ShapeDtypeStruct((128, ab), f32),
        in_specs=[any_space, any_space, any_space],
        out_specs=pl.BlockSpec(memory_space=pltpu.VMEM),
        scratch_shapes=scratch,
        compiler_params=pltpu.CompilerParams(collective_id=0, has_side_effects=True, vmem_limit_bytes=60 << 20),
        name="ladder",
    )(buf, inv, integrals)


def shards(lam_tiles, lam_ids, integrals):
    _, s_count, pairs, tile = lam_tiles.shape
    buf, inv = bucket(lam_ids, lam_tiles.reshape(s_count, pairs, tile), lax.axis_size("col"))
    return ladder(buf, inv, integrals)


def solution(mesh):
    return jax.shard_map(
        shards,
        mesh=mesh,
        in_specs=(P(("row", "col"), None, None, None), P(("row", "col"), None), P("row", "col")),
        out_specs=P("col", "row"),
        check_vma=False,
    )
```

time: 92.7 us -> 87.7 us (0.946)
  the two profiles are of different devices: /device:TPU:65 before, /device:TPU:22 now
where the time goes in v3:
time: 87.7 us; the launch traced here: 87.5 us
  Pallas kernels  85.6 us (98%)
  local copies, waits for them, and re-layouts  1.89 us (2%)
    pallas_call x1, Pallas kernels, ladder(): pl.pallas_call(ladder_kernel, out_shape=jax.ShapeDtypeStruct((128, ab), f...  81.9 us
    pallas_call x1, Pallas kernels, bucket(): pl.pallas_call(bucket_kernel, out_shape=(jax.ShapeDtypeStruct((n_col * CA...  3.76 us
    unnamed x1, local copies, waits for them, and re-layouts  1.89 us

profile of v3, /device:TPU:22, one launch (start us, length us, event | category | flops | bytes accessed | tf_op | source)
XLA Modules:
  0.0 87.5 jit_solution(5947558710925962568)
XLA Ops:
  0.0 3.8 %bucket.1 = (bf16[256,16,128]{2,1,0:T(8,128)(2,1)}, s32[16,1,128]{2,1,0:T(1,128)}) custom-call(s32[1,128]{1,0:T(1,128)} %ids_ref.1, bf16[128,16,128]{2,1,0:T(8,128)(2,1)} %bitcast.1), custom_call_target="tpu_custom_call" | custom-call | tf_op jit(solution)/shard_map/bucket/pallas_call | solution.py:54
  3.8 81.9 %ladder.1 = f32[128,1024]{1,0:T(8,128)} custom-call(bf16[256,16,128]{2,1,0:T(8,128)(2,1)} %get-tuple-element.7.buf_ref, s32[16,1,128]{2,1,0:T(1,128)} %get-tuple-element.8.inv_ref, bf16[1024,4096]{1,0:T(8,128)(2,1)} %int_ref.1), custom_call_target="tpu_custom_call" | custom-call | tf_op jit(solution)/shard_map/ladder/pallas_call | solution.py:590
  85.6 1.9 %copy.5 = f32[128,1024]{1,0:T(8,128)} copy(f32[128,1024]{1,0:T(8,128)} %ladder.1) | data formatting | bytes 1048576

commit v4 on v3

--- a/solution.py
+++ b/solution.py
@@ -25,10 +25,12 @@
 GROUPS = {"L": (0, 256), "M": (256, 256), "N": (512, 512)}
 
 
-def bucket_kernel(ids_ref, lam_ref, out_ref, inv_ref, used):
+def bucket_kernel(ids_ref, lam_ref, out_ref, inv_ref, used, place, tiles, sem):
     n_col, _, _ = inv_ref.shape
     kt = 32
-    first = lax.axis_index("col") * CAP
+    own = lax.axis_index("col") * CAP
+    load = pltpu.make_async_copy(lam_ref, tiles, sem)
+    load.start()
 
     def clear(b, carry):
         used[b] = 0
@@ -38,16 +40,23 @@
 
     lax.fori_loop(0, n_col, clear, 0)
 
-    def body(s, carry):
+    def find(s, carry):
         tile = ids_ref[0, s]
         b = tile // kt
         slot = used[b]
         used[b] = slot + 1
-        inv_ref[b, 0, tile % kt] = first + slot
-        out_ref[b * CAP + slot] = lam_ref[s]
-        return carry
-
-    lax.fori_loop(0, lam_ref.shape[0], body, 0, unroll=8)
+        inv_ref[b, 0, tile % kt] = own + slot
+        place[s] = b * CAP + slot
+        return carry
+
+    lax.fori_loop(0, tiles.shape[0], find, 0, unroll=8)
+    load.wait()
+
+    def put(s, carry):
+        out_ref[place[s]] = tiles[s]
+        return carry
+
+    lax.fori_loop(0, tiles.shape[0], put, 0, unroll=8)
 
 
 def bucket(ids, tiles, n_col):
@@ -59,13 +68,18 @@
         ),
         in_specs=[
             pl.BlockSpec(memory_space=pltpu.SMEM),
-            pl.BlockSpec(memory_space=pltpu.VMEM),
+            pl.BlockSpec(memory_space=pl.ANY),
         ],
         out_specs=(
             pl.BlockSpec(memory_space=pltpu.VMEM),
             pl.BlockSpec(memory_space=pltpu.SMEM),
         ),
-        scratch_shapes=[pltpu.SMEM((n_col,), jnp.int32)],
+        scratch_shapes=[
+            pltpu.SMEM((n_col,), jnp.int32),
+            pltpu.SMEM((tiles.shape[0],), jnp.int32),
+            pltpu.VMEM(tiles.shape, tiles.dtype),
+            pltpu.SemaphoreType.DMA,
+        ],
         name="bucket",
     )(ids, tiles)
 
@@ -464,14 +478,13 @@
     pass_on(1, DYS[2:])
     build_all(B, 0)
     run(B, 0)
-    pass_sums(OWN, "L")
-    pass_sums(OWN, "M")
     pass_sums(A, "N")
     arrived(PB, d_recv.at[1])
     build_all(PB, 1)
     run(PB, 1)
-    pass_sums(PART, "L")
-    pass_sums(PART, "M")
+    for step in (OWN, PART, A):
+        pass_sums(step, "L")
+        pass_sums(step, "M")
     pass_sums(PA, "N")
     pass_far(DYS)
     wait_bytes(tabs.at[PZ2], t_recv.at[PZ2])
@@ -480,21 +493,19 @@
     run(Z2, 0)
     pass_sums(B, "N")
     pass_sums(B, "M")
-    pass_sums(A, "L")
+    pass_sums(PA, "L")
+    pass_sums(PA, "M")
     arrived(PZ2, d_recv.at[2])
     fetch(PZ2).wait()
     build_all(PZ2, 1)
     product(1, 1)
     send(PZ2, "N")
-    pass_sums(A, "M")
+    pass_sums(B, "L")
     product(1, 0)
     send(PZ2, "L")
     send(PZ2, "M")
-    pass_sums(PA, "L")
-    pass_sums(PA, "M")
     pass_sums(PB, "N")
     pass_sums(PB, "M")
-    pass_sums(B, "L")
     pass_sums(Z2, "N")
     pass_sums(PB, "L")
     pass_sums(Z2, "L")
@@ -589,7 +600,7 @@
     any_space = pl.BlockSpec(memory_space=pl.ANY)
     return pl.pallas_call(
         ladder_kernel,
-        out_shape=jax.ShapeDtypeStruct((128, ab), f32),
+        out_shape=vmem((128, ab), f32),
         in_specs=[any_space, any_space, any_space],
         out_specs=pl.BlockSpec(memory_space=pltpu.VMEM),
         scratch_shapes=scratch,

time: 87.7 us -> 88.5 us (level)
  Pallas kernels: 85.6 us -> 87.6 us
  local copies, waits for them, and re-layouts: 1.89 us -> 0.8 us
    pallas_call x1, Pallas kernels: 81.9 us -> 84 us  [ladder(): pl.pallas_call(ladder_kernel, out_shape=vmem((128, ab), f32), in_specs=[a...]
    unnamed x1, local copies, waits for them, and re-layouts: 1.89 us -> 0.8 us
where the time goes in v4:
time: 88.5 us; the launch traced here: 88.4 us
  Pallas kernels  87.6 us (99%)
    pallas_call x1, Pallas kernels, ladder(): pl.pallas_call(ladder_kernel, out_shape=vmem((128, ab), f32), in_specs=[a...  84 us
    pallas_call x1, Pallas kernels, bucket(): pl.pallas_call(bucket_kernel, out_shape=(jax.ShapeDtypeStruct((n_col * CA...  3.56 us

profile of v4, /device:TPU:22, one launch (start us, length us, event | category | flops | bytes accessed | tf_op | source)
XLA Modules:
  0.0 88.4 jit_solution(847027247883076510)
XLA Ops:
  0.0 3.6 %bucket.1 = (bf16[256,16,128]{2,1,0:T(8,128)(2,1)}, s32[16,1,128]{2,1,0:T(1,128)}) custom-call(s32[1,128]{1,0:T(1,128)} %ids_ref.1, bf16[128,16,128]{2,1,0:T(8,128)(2,1)} %bitcast.1), custom_call_target="tpu_custom_call" | custom-call | tf_op jit(solution)/shard_map/bucket/pallas_call | solution.py:63
  3.6 84.0 %ladder.1 = f32[128,1024]{1,0:T(8,128)S(1)} custom-call(bf16[256,16,128]{2,1,0:T(8,128)(2,1)} %get-tuple-element.7.buf_ref, s32[16,1,128]{2,1,0:T(1,128)} %get-tuple-element.8.inv_ref, bf16[1024,4096]{1,0:T(8,128)(2,1)} %int_ref.1), custom_call_target="tpu_custom_call" | custom-call | tf_op jit(solution)/shard_map/ladder/pallas_call | solution.py:601
  87.6 0.8 copy.5
